TPU v7x, 32 devices: a whole 2x2x4 slice. The times are simulated.
32 devices in a mesh: freq: 4 (over y, core), src: 8 (over z, x).
Axes of the slice: x: 2, y: 2, z: 4, core: 2. Of those that a mesh axis runs over, the one named last changes fastest.
Arguments:
- spectra: bfloat16 [8, 2, 306, 512], P('freq', None, None, 'src'), may hold values from -200 to 200
- keep: int32 [512], P('src'), may hold values from 0 to 1, as said below
- lead_field: float32 [3, 306, 2048], P(None, None, 'src'), may hold values from -0.625 to 0.625
- parcel: int32 [2048], P('src'), may hold values from 0 to 67, never falling along the last dimension, each value on 1 to 61 neighbouring positions
Outputs:
- source_power: float32 [8, 2048], P('freq', 'src')
- parcel_power: float32 [8, 68], P('freq')
Inputs may be any that keep to these rules, and one draw needn't show every extreme that they name: `keep`: at least 8 epochs are kept.
All inputs are finite; a program needn't handle non-finite values.
Results may differ from a plain program's by a relative error of at most 0.0003.
Values sent between devices are 32-bit elements; how exact they have to be, the bound alone decides.
A program may use at most 64 MiB of HBM per device.

v0:
```python
import functools
import jax
import jax.numpy as jnp
from jax import lax
from jax.experimental import pallas as pl
from jax.experimental.pallas import tpu as pltpu
from jax.sharding import PartitionSpec as P

PARCELS = 68
ridge = 0.05
MESH = pl.DeviceIdType.MESH
HI = lax.Precision.HIGHEST
LANES = 128


def block_plan(rows):
    sizes = [min(LANES, rows - at) for at in range(0, rows, LANES)]
    offsets, total = {}, 0
    for i, size in enumerate(sizes):
        for j in range(i + 1):
            offsets[i, j] = total
            total += size // 8
    return sizes, offsets, total


def cov_kernel(n, chunk, x_ref, out_ref, packed, landing, gathered, send, recv, send2, recv2):
    bins, rows, _ = x_ref.shape
    sizes, offsets, total = block_plan(rows)
    me = lax.axis_index("src")
    barrier = pltpu.get_barrier_semaphore()
    for d in range(1, n):
        pl.semaphore_signal(barrier, inc=1, device_id={"src": lax.rem(me + d, n)}, device_id_type=MESH)
    for f in range(bins):
        for i, size in enumerate(sizes):
            left = x_ref[f, i * LANES : i * LANES + size, :]
            for j in range(i + 1):
                width = sizes[j]
                right = x_ref[f, j * LANES : j * LANES + width, :]
                block = lax.dot_general(left, right, (((1,), (1,)), ((), ())), preferred_element_type=jnp.float32)
                if width < LANES:
                    block = jnp.concatenate([block, jnp.zeros((size, LANES - width), jnp.float32)], axis=1)
                at = f * total + offsets[i, j]
                packed[at : at + size // 8] = block.reshape(size // 8, 8, LANES)
    spare = n * chunk - bins * total
    if spare:
        packed[bins * total :] = jnp.zeros((spare, 8, LANES), jnp.float32)
    pl.semaphore_wait(barrier, n - 1)
    copies = []
    for d in range(1, n):
        to = lax.rem(me + d, n)
        copy = pltpu.make_async_remote_copy(
            src_ref=packed.at[pl.ds(to * chunk, chunk)],
            dst_ref=landing.at[d],
            send_sem=send.at[d],
            recv_sem=recv.at[d],
            device_id={"src": to},
            device_id_type=MESH,
        )
        copy.start()
        copies.append(copy)
    acc = packed[pl.ds(me * chunk, chunk)]
    for d in range(1, n):
        copies[d - 1].wait_recv()
        acc = acc + landing[d]
    gathered[pl.ds(me * chunk, chunk)] = acc
    again = []
    for d in range(1, n):
        to = lax.rem(me + d, n)
        copy = pltpu.make_async_remote_copy(
            src_ref=gathered.at[pl.ds(me * chunk, chunk)],
            dst_ref=gathered.at[pl.ds(me * chunk, chunk)],
            send_sem=send2.at[d],
            recv_sem=recv2.at[d],
            device_id={"src": to},
            device_id_type=MESH,
        )
        copy.start()
        again.append(copy)
    for d in range(1, n):
        again[d - 1].wait_recv()
    for d in range(1, n):
        copies[d - 1].wait_send()
        again[d - 1].wait_send()
    out_ref[...] = gathered[...]


def summed_cov(x, n):
    bins, rows, _ = x.shape
    total = block_plan(rows)[2] * bins
    chunk = -(-total // n)
    full = (n * chunk, 8, LANES)
    return pl.pallas_call(
        functools.partial(cov_kernel, n, chunk),
        out_shape=jax.ShapeDtypeStruct(full, jnp.float32),
        in_specs=[pl.BlockSpec(memory_space=pltpu.VMEM)],
        out_specs=pl.BlockSpec(memory_space=pltpu.VMEM),
        scratch_shapes=[
            pltpu.VMEM(full, jnp.float32),
            pltpu.VMEM((n, chunk, 8, LANES), jnp.float32),
            pltpu.VMEM(full, jnp.float32),
            pltpu.SemaphoreType.DMA((n,)),
            pltpu.SemaphoreType.DMA((n,)),
            pltpu.SemaphoreType.DMA((n,)),
            pltpu.SemaphoreType.DMA((n,)),
        ],
        compiler_params=pltpu.CompilerParams(collective_id=0, has_side_effects=True),
        name="cov_exchange",
    )(x)


def split3(x):
    high = x.astype(jnp.bfloat16).astype(jnp.float32)
    rest = x - high
    middle = rest.astype(jnp.bfloat16).astype(jnp.float32)
    return high, middle, rest - middle


def panel(p):
    lane = lax.broadcasted_iota(jnp.int32, (8, LANES), 1)
    row = lax.broadcasted_iota(jnp.int32, (8, LANES), 0)
    for k in range(8):
        col = jnp.broadcast_to(p[:, k : k + 1], (8, LANES))
        pivot = jnp.broadcast_to(col[k : k + 1, :], (8, LANES))
        line = jnp.where(lane == k, 1.0, jnp.broadcast_to(p[k : k + 1, :], (8, LANES)))
        scale = lax.rsqrt(pivot)
        scale = scale * (1.5 - 0.5 * pivot * scale * scale)
        line = line * scale
        step = jnp.where(row > k, col * scale, 0.0)
        p = jnp.where(row == k, line, jnp.where((lane == k) & (row > k), 0.0, p) - step * line)
    return jnp.where((lane < 8) & (lane > row), 0.0, p)


def invert_factors(work, bins, size):
    lane = lax.broadcasted_iota(jnp.int32, (8, LANES), 1)
    rest_lane = lax.broadcasted_iota(jnp.int32, (size - 8, LANES), 1)

    def body(t, carry):
        for f in range(bins):
            u = panel(work[f, 0:8, :])
            ahead = jnp.where((lane >= 8) & (lane < size - 8 * t), u, 0.0)
            ah, am, al = split3(ahead)
            uh, um, ul = split3(u)
            left = jnp.concatenate([ah, ah, am, ah, am, al], axis=0).astype(jnp.bfloat16)
            right = jnp.concatenate([uh, um, uh, ul, um, uh], axis=0).astype(jnp.bfloat16)
            update = lax.dot_general(left, right, (((0,), (0,)), ((), ())), preferred_element_type=jnp.float32)
            below = jnp.where(rest_lane < 8, 0.0, work[f, 8:size, :]) - update[8:size, :]
            work[f, 0 : size - 8, :] = pltpu.roll(below, LANES - 8, axis=1)
            work[f, size - 8 : size, :] = pltpu.roll(u, LANES - 8, axis=1)
        return carry

    lax.fori_loop(0, size // 8, body, 0)
    if size < LANES:
        for f in range(bins):
            work[f, 0:size, :] = pltpu.roll(work[f, 0:size, :], size, axis=1)


def dot(a, b):
    return jnp.dot(a, b, precision=HI, preferred_element_type=jnp.float32)


def dot_t(a, b):
    return lax.dot_general(a, b, (((1,), (1,)), ((), ())), precision=HI, preferred_element_type=jnp.float32)


def solve_kernel(bins, packed_ref, lead_ref, out_ref, blocks, work, white, tail):
    channels, sources = lead_ref.shape[1], lead_ref.shape[2]
    rows = blocks_rows(channels)
    sizes, offsets, total = block_plan(rows)
    count = len(sizes)
    for f in range(bins):
        def raw(i, j):
            at = f * total + offsets[i, j]
            return packed_ref[at : at + sizes[i] // 8].reshape(sizes[i], LANES)

        spot = f * total + offsets[count - 1, count - 1]
        edge = channels - (count - 1) * LANES
        kept = packed_ref[spot + edge // 8][edge % 8 : edge % 8 + 1, edge : edge + 1]
        inverse_kept = 1.0 / kept
        eyes, trace = [], jnp.zeros((1, 1), jnp.float32)
        for i, size in enumerate(sizes):
            r = lax.broadcasted_iota(jnp.int32, (size, LANES), 0)
            c = lax.broadcasted_iota(jnp.int32, (size, LANES), 1)
            inside = r + i * LANES < channels
            diagonal = jnp.where((r == c) & inside, raw(i, i), 0.0)
            trace = trace + jnp.sum(jnp.sum(diagonal, axis=0, keepdims=True), axis=1, keepdims=True)
        add = ridge * (trace * inverse_kept) / channels
        for i, size in enumerate(sizes):
            r = lax.broadcasted_iota(jnp.int32, (size, LANES), 0)
            c = lax.broadcasted_iota(jnp.int32, (size, LANES), 1)
            inside = r + i * LANES < channels
            for j in range(i + 1):
                value = raw(i, j) * inverse_kept
                value = jnp.where(inside & (c + j * LANES < channels), value, 0.0)
                if i == j:
                    value = value + jnp.where(r == c, jnp.where(inside, add, 1.0), 0.0)
                blocks[f, i, j, 0:size, :] = value

    tail[...] = jnp.zeros_like(tail)
    for o in range(3):
        tail[0 : channels - (count - 1) * LANES, o * sources : (o + 1) * sources] = lead_ref[o, (count - 1) * LANES : channels, :]

    def lead_block(i):
        if i == count - 1:
            return tail[...]
        return jnp.concatenate([lead_ref[o, i * LANES : (i + 1) * LANES, :] for o in range(3)], axis=1)

    for i, size in enumerate(sizes):
        for f in range(bins):
            work[f, 0:size, :] = blocks[f, i, i, 0:size, :]
        invert_factors(work, bins, size)
        for f in range(bins):
            inverse = work[f, 0:size, 0:size]
            for j in range(i + 1, count):
                blocks[f, j, i, 0 : sizes[j], :] = dot_t(blocks[f, j, i, 0 : sizes[j], :], inverse)
            for j in range(i + 1, count):
                for k in range(i + 1, j + 1):
                    low, high = blocks[f, j, i, 0 : sizes[j], :], blocks[f, k, i, 0 : sizes[k], :]
                    blocks[f, j, k, 0 : sizes[j], 0 : sizes[k]] = blocks[f, j, k, 0 : sizes[j], 0 : sizes[k]] - dot_t(low, high)
            column = lead_block(i)
            for j in range(i):
                column = column - dot(blocks[f, i, j, 0:size, :], white[f, j * LANES : (j + 1) * LANES, :])
            white[f, i * LANES : i * LANES + size, :] = dot(inverse, column)
    for f in range(bins):
        gram = {}
        for a in range(3):
            for b in range(a, 3):
                wa = white[f, :, a * sources : (a + 1) * sources]
                wb = white[f, :, b * sources : (b + 1) * sources]
                gram[a, b] = jnp.sum(wa * wb, axis=0, keepdims=True)
        xx, xy, xz, yy, yz, zz = gram[0, 0], gram[0, 1], gram[0, 2], gram[1, 1], gram[1, 2], gram[2, 2]
        minor_xx = yy * zz - yz * yz
        minor_yy = xx * zz - xz * xz
        minor_zz = xx * yy - xy * xy
        determinant = xx * minor_xx - xy * (xy * zz - yz * xz) + xz * (xy * yz - yy * xz)
        out_ref[f : f + 1, :] = (minor_xx + minor_yy + minor_zz) / determinant


def blocks_rows(channels):
    return -(-(channels + 1) // 16) * 16


def solve(packed, lead_field, bins):
    channels, sources = lead_field.shape[1:]
    rows = blocks_rows(channels)
    sizes, _, _ = block_plan(rows)
    count = len(sizes)
    return pl.pallas_call(
        functools.partial(solve_kernel, bins),
        out_shape=jax.ShapeDtypeStruct((bins, sources), jnp.float32),
        in_specs=[pl.BlockSpec(memory_space=pltpu.VMEM)] * 2,
        out_specs=pl.BlockSpec(memory_space=pltpu.VMEM),
        scratch_shapes=[
            pltpu.VMEM((bins, count, count, LANES, LANES), jnp.float32),
            pltpu.VMEM((bins, LANES, LANES), jnp.float32),
            pltpu.VMEM((bins, rows, 3 * sources), jnp.float32),
            pltpu.VMEM((sizes[-1], 3 * sources), jnp.float32),
        ],
        name="factor_whiten",
    )(packed, lead_field)


def parcel_kernel(nf, ns, power_ref, parcel_ref, out_ref, mine, bin_land, part, part_land, send_f, recv_f, send_s, recv_s):
    bins, sources = power_ref.shape
    mf, ms = lax.axis_index("freq"), lax.axis_index("src")
    barrier = pltpu.get_barrier_semaphore()
    for d in range(1, nf):
        pl.semaphore_signal(barrier, inc=1, device_id={"freq": lax.rem(mf + d, nf)}, device_id_type=MESH)
    for d in range(1, ns):
        pl.semaphore_signal(barrier, inc=1, device_id={"src": lax.rem(ms + d, ns)}, device_id_type=MESH)
    power = power_ref[...]
    here = jnp.sum(power, axis=0, keepdims=True)
    mine[...] = jnp.broadcast_to(here, mine.shape)
    pl.semaphore_wait(barrier, nf + ns - 2)
    copies = []
    for d in range(1, nf):
        copy = pltpu.make_async_remote_copy(
            src_ref=mine,
            dst_ref=bin_land.at[d],
            send_sem=send_f.at[d],
            recv_sem=recv_f.at[d],
            device_id={"freq": lax.rem(mf + d, nf)},
            device_id_type=MESH,
        )
        copy.start()
        copies.append(copy)
    member = lax.broadcasted_iota(jnp.int32, (LANES, sources), 0) == parcel_ref[...]
    onehot = jnp.where(member, 1.0, 0.0)
    total = here
    for d in range(1, nf):
        copies[d - 1].wait_recv()
        total = total + bin_land[d][0:1, :]
    relative = power / (total / (bins * nf))
    stacked = jnp.concatenate([relative, jnp.ones((8 - bins, sources), jnp.float32)], axis=0)
    sums = dot_t(stacked, onehot)
    part[...] = sums
    again = []
    for d in range(1, ns):
        copy = pltpu.make_async_remote_copy(
            src_ref=part,
            dst_ref=part_land.at[d],
            send_sem=send_s.at[d],
            recv_sem=recv_s.at[d],
            device_id={"src": lax.rem(ms + d, ns)},
            device_id_type=MESH,
        )
        copy.start()
        again.append(copy)
    part_land[0] = sums
    for d in range(1, ns):
        again[d - 1].wait_recv()
    whole = jnp.zeros_like(sums)
    for place in range(ns):
        whole = whole + part_land[lax.rem(ms - place + ns, ns)]
    for copy in copies + again:
        copy.wait_send()
    out_ref[...] = whole[0:bins, 0:PARCELS] / whole[bins : bins + 1, 0:PARCELS]


def parcel_power(power, parcel, nf, ns):
    bins, sources = power.shape
    return pl.pallas_call(
        functools.partial(parcel_kernel, nf, ns),
        out_shape=jax.ShapeDtypeStruct((bins, PARCELS), jnp.float32),
        in_specs=[pl.BlockSpec(memory_space=pltpu.VMEM)] * 2,
        out_specs=pl.BlockSpec(memory_space=pltpu.VMEM),
        scratch_shapes=[
            pltpu.VMEM((8, sources), jnp.float32),
            pltpu.VMEM((nf, 8, sources), jnp.float32),
            pltpu.VMEM((8, LANES), jnp.float32),
            pltpu.VMEM((ns, 8, LANES), jnp.float32),
            pltpu.SemaphoreType.DMA((nf,)),
            pltpu.SemaphoreType.DMA((nf,)),
            pltpu.SemaphoreType.DMA((ns,)),
            pltpu.SemaphoreType.DMA((ns,)),
        ],
        compiler_params=pltpu.CompilerParams(collective_id=1, has_side_effects=True),
        name="parcel_exchange",
    )(power, parcel)


def epoch_rows(spectra, keep):
    bins, parts, channels, epochs = spectra.shape
    kept = keep.astype(jnp.bfloat16)
    masked = spectra * kept
    x = jnp.transpose(masked, (0, 2, 1, 3)).reshape(bins, channels, parts * epochs)
    count = jnp.concatenate([kept, jnp.zeros(((parts - 1) * epochs,), jnp.bfloat16)])
    count = jnp.broadcast_to(count[None, None, :], (bins, 1, parts * epochs))
    rows = blocks_rows(channels)
    spare = jnp.zeros((bins, rows - channels - 1, parts * epochs), jnp.bfloat16)
    return jnp.concatenate([x, count, spare], axis=1)


def local(nf, ns, spectra, keep, lead_field, parcel):
    bins = spectra.shape[0]
    packed = summed_cov(epoch_rows(spectra, keep), ns)
    power = solve(packed, lead_field, bins)
    return power, parcel_power(power, parcel[None, :], nf, ns)


def solution(mesh):
    in_specs = (P("freq", None, None, "src"), P("src"), P(None, None, "src"), P("src"))
    out_specs = (P("freq", "src"), P("freq", None))
    body = functools.partial(local, mesh.shape["freq"], mesh.shape["src"])
    return jax.shard_map(body, mesh=mesh, in_specs=in_specs, out_specs=out_specs, check_vma=False)
```

profile of v0, /device:TPU:0, one launch (start us, length us, event | category | flops | bytes accessed | tf_op | source)
XLA Modules:
  0.0 138.2 jit_solution(5641704271364482489)
XLA Ops:
  0.6 0.0 copy-start
  0.6 0.6 copy-done
  1.3 0.1 pad.3.clone
  1.4 1.0 broadcast_multiply_fusion
  2.4 0.2 copy.7
  2.6 0.8 maximum_maximum_fusion.x_ref
  3.4 33.5 %cov_exchange.1.packed_ref = f32[144,8,128]{2,1,0:T(8,128)} custom-call(bf16[2,320,128]{2,1,0:T(8,128)(2,1)} %maximum_maximum_fusion.x_ref), custom_call_target="tpu_custom_call" | custom-call | tf_op jit(solution)/shard_map/cov_exchange/pallas_call | solution.py:92
  36.9 86.2 %factor_whiten.1.power_ref = f32[2,256]{1,0:T(2,128)} custom-call(f32[144,8,128]{2,1,0:T(8,128)} %cov_exchange.1.packed_ref, f32[3,306,256]{2,1,0:T(8,128)} %lead_ref.1), custom_call_target="tpu_custom_call" | custom-call | tf_op jit(solution)/shard_map/factor_whiten/pallas_call | solution.py:247
  123.1 13.9 %parcel_exchange.1 = f32[2,68]{1,0:T(2,128)} custom-call(f32[2,256]{1,0:T(2,128)} %factor_whiten.1.power_ref, s32[1,256]{1,0:T(1,128)} %bitcast.5), custom_call_target="tpu_custom_call" | custom-call | tf_op jit(solution)/shard_map/parcel_exchange/pallas_call | solution.py:321
  136.9 1.2 copy.9
  (4 shorter events, 0.0 us)
Async XLA Ops:
  0.6 0.7 copy-start
where the time goes:
time: 138 us
  Pallas kernels  134 us (97%)
  local copies, waits for them, and re-layouts  2.14 us (2%)
  other arithmetic  1.81 us (1%)
    pallas_call x1, Pallas kernels, solve(): pl.pallas_call(functools.partial(solve_kernel, bins), out_shape=jax.Shape...  86.2 us
    pallas_call x1, Pallas kernels, summed_cov(): pl.pallas_call(functools.partial(cov_kernel, n, chunk), out_shape=jax.Sha...  33.5 us
    pallas_call x1, Pallas kernels, parcel_power(): pl.pallas_call(functools.partial(parcel_kernel, nf, ns), out_shape=jax.Sh...  13.9 us

commit v1 on v0

--- a/solution.py
+++ b/solution.py
@@ -115,19 +115,23 @@
     return high, middle, rest - middle
 
 
-def panel(p):
+def panels(ps):
     lane = lax.broadcasted_iota(jnp.int32, (8, LANES), 1)
     row = lax.broadcasted_iota(jnp.int32, (8, LANES), 0)
     for k in range(8):
-        col = jnp.broadcast_to(p[:, k : k + 1], (8, LANES))
-        pivot = jnp.broadcast_to(col[k : k + 1, :], (8, LANES))
-        line = jnp.where(lane == k, 1.0, jnp.broadcast_to(p[k : k + 1, :], (8, LANES)))
-        scale = lax.rsqrt(pivot)
-        scale = scale * (1.5 - 0.5 * pivot * scale * scale)
-        line = line * scale
-        step = jnp.where(row > k, col * scale, 0.0)
-        p = jnp.where(row == k, line, jnp.where((lane == k) & (row > k), 0.0, p) - step * line)
-    return jnp.where((lane < 8) & (lane > row), 0.0, p)
+        done = []
+        for p in ps:
+            col = jnp.where(row >= k, jnp.broadcast_to(p[:, k : k + 1], (8, LANES)), 0.0)
+            pivot = jnp.broadcast_to(col[k : k + 1, :], (8, LANES))
+            line = jnp.where(lane == k, 1.0, jnp.broadcast_to(p[k : k + 1, :], (8, LANES)))
+            scale = lax.rsqrt(pivot)
+            scale = scale * (1.5 - (0.5 * pivot) * (scale * scale))
+            line = line * scale
+            step = col * scale
+            below = jnp.where((lane == k) & (row > k), 0.0, p) - step * line
+            done.append(jnp.where(row > k, below, jnp.where(row == k, line, p)))
+        ps = done
+    return [jnp.where((lane < 8) & (lane > row), 0.0, p) for p in ps]
 
 
 def invert_factors(work, bins, size):
@@ -135,17 +139,23 @@
     rest_lane = lax.broadcasted_iota(jnp.int32, (size - 8, LANES), 1)
 
     def body(t, carry):
-        for f in range(bins):
-            u = panel(work[f, 0:8, :])
+        us = panels([work[f, 0:8, :] for f in range(bins)])
+        updates = []
+        for u in us:
             ahead = jnp.where((lane >= 8) & (lane < size - 8 * t), u, 0.0)
             ah, am, al = split3(ahead)
             uh, um, ul = split3(u)
             left = jnp.concatenate([ah, ah, am, ah, am, al], axis=0).astype(jnp.bfloat16)
             right = jnp.concatenate([uh, um, uh, ul, um, uh], axis=0).astype(jnp.bfloat16)
-            update = lax.dot_general(left, right, (((0,), (0,)), ((), ())), preferred_element_type=jnp.float32)
-            below = jnp.where(rest_lane < 8, 0.0, work[f, 8:size, :]) - update[8:size, :]
-            work[f, 0 : size - 8, :] = pltpu.roll(below, LANES - 8, axis=1)
-            work[f, size - 8 : size, :] = pltpu.roll(u, LANES - 8, axis=1)
+            updates.append(
+                lax.dot_general(left, right, (((0,), (0,)), ((), ())), preferred_element_type=jnp.float32)
+            )
+        below = [jnp.where(rest_lane < 8, 0.0, work[f, 8:size, :]) - updates[f][8:size, :] for f in range(bins)]
+        below = [pltpu.roll(x, LANES - 8, axis=1) for x in below]
+        last = [pltpu.roll(u, LANES - 8, axis=1) for u in us]
+        for f in range(bins):
+            work[f, 0 : size - 8, :] = below[f]
+            work[f, size - 8 : size, :] = last[f]
         return carry
 
     lax.fori_loop(0, size // 8, body, 0)

time: 138 us -> 97.8 us (0.71)
  Pallas kernels: 134 us -> 93 us
    pallas_call x1, Pallas kernels: 86.2 us -> 45.6 us  [solve(): pl.pallas_call(functools.partial(solve_kernel, bins), out_shape=jax.Shape...]
where the time goes in v1:
time: 97.8 us; the launch traced here: 97.6 us
  Pallas kernels  93 us (95%)
  local copies, waits for them, and re-layouts  2.14 us (2%)
  other arithmetic  1.81 us (2%)
    pallas_call x1, Pallas kernels, solve(): pl.pallas_call(functools.partial(solve_kernel, bins), out_shape=jax.Shape...  45.6 us
    pallas_call x1, Pallas kernels, summed_cov(): pl.pallas_call(functools.partial(cov_kernel, n, chunk), out_shape=jax.Sha...  33.5 us
    pallas_call x1, Pallas kernels, parcel_power(): pl.pallas_call(functools.partial(parcel_kernel, nf, ns), out_shape=jax.Sh...  13.9 us

profile of v1, /device:TPU:0, one launch (start us, length us, event | category | flops | bytes accessed | tf_op | source)
XLA Modules:
  0.0 97.6 jit_solution(9372620315569458998)
XLA Ops:
  0.6 0.0 copy-start
  0.6 0.6 copy-done
  1.3 0.1 pad.3.clone
  1.4 1.0 %broadcast_multiply_fusion = bf16[2,2,306,64]{2,3,1,0:T(8,128)(2,1)S(1)} fusion(bf16[2,2,306,64]{2,3,1,0:T(8,128)(2,1)} %param.4, bf16[64]{0:T(256)(128)(2,1)S(1)} %convert_element_type.3), kind=kLoop, calls=%fused_computation.1 | loop fusion | flops 78336 | bytes 313472 | tf_op jit(solution)/shard_map/mul | solution.py:354
  2.4 0.2 copy.7
  2.6 0.8 maximum_maximum_fusion.x_ref
  3.4 33.5 %cov_exchange.1.packed_ref = f32[144,8,128]{2,1,0:T(8,128)} custom-call(bf16[2,320,128]{2,1,0:T(8,128)(2,1)} %maximum_maximum_fusion.x_ref), custom_call_target="tpu_custom_call" | custom-call | tf_op jit(solution)/shard_map/cov_exchange/pallas_call | solution.py:92
  36.9 45.6 %factor_whiten.1.power_ref = f32[2,256]{1,0:T(2,128)} custom-call(f32[144,8,128]{2,1,0:T(8,128)} %cov_exchange.1.packed_ref, f32[3,306,256]{2,1,0:T(8,128)} %lead_ref.1), custom_call_target="tpu_custom_call" | custom-call | tf_op jit(solution)/shard_map/factor_whiten/pallas_call | solution.py:257
  82.5 13.9 %parcel_exchange.1 = f32[2,68]{1,0:T(2,128)} custom-call(f32[2,256]{1,0:T(2,128)} %factor_whiten.1.power_ref, s32[1,256]{1,0:T(1,128)} %bitcast.5), custom_call_target="tpu_custom_call" | custom-call | tf_op jit(solution)/shard_map/parcel_exchange/pallas_call | solution.py:331
  96.4 1.2 %copy.9 = f32[2,68]{1,0:T(2,128)} copy(f32[2,68]{1,0:T(2,128)} %parcel_exchange.1) | data formatting | bytes 1088
  (4 shorter events, 0.0 us)
Async XLA Ops:
  0.6 0.7 copy-start

commit v2 on v1

--- a/solution.py
+++ b/solution.py
@@ -134,12 +134,31 @@
     return [jnp.where((lane < 8) & (lane > row), 0.0, p) for p in ps]
 
 
+def next_rows(u):
+    row = lax.broadcasted_iota(jnp.int32, (8, LANES), 0)
+    rows = jnp.zeros((8, LANES), jnp.float32)
+    for j in range(8):
+        product = jnp.broadcast_to(u[:, 8 + j : 9 + j], (8, LANES)) * u
+        rows = jnp.where(row == j, jnp.sum(product, axis=0, keepdims=True), rows)
+    return rows
+
+
 def invert_factors(work, bins, size):
     lane = lax.broadcasted_iota(jnp.int32, (8, LANES), 1)
     rest_lane = lax.broadcasted_iota(jnp.int32, (size - 8, LANES), 1)
 
-    def body(t, carry):
-        us = panels([work[f, 0:8, :] for f in range(bins)])
+    def store(us, updates):
+        below = [jnp.where(rest_lane < 8, 0.0, work[f, 8:size, :]) for f in range(bins)]
+        if updates is not None:
+            below = [x - update[8:size, :] for x, update in zip(below, updates)]
+        below = [pltpu.roll(x, LANES - 8, axis=1) for x in below]
+        last = [pltpu.roll(u, LANES - 8, axis=1) for u in us]
+        for f in range(bins):
+            work[f, 0 : size - 8, :] = below[f]
+            work[f, size - 8 : size, :] = last[f]
+
+    def body(t, us):
+        heads = [jnp.where(lane < 8, 0.0, work[f, 8:16, :]) - next_rows(us[f]) for f in range(bins)]
         updates = []
         for u in us:
             ahead = jnp.where((lane >= 8) & (lane < size - 8 * t), u, 0.0)
@@ -150,15 +169,12 @@
             updates.append(
                 lax.dot_general(left, right, (((0,), (0,)), ((), ())), preferred_element_type=jnp.float32)
             )
-        below = [jnp.where(rest_lane < 8, 0.0, work[f, 8:size, :]) - updates[f][8:size, :] for f in range(bins)]
-        below = [pltpu.roll(x, LANES - 8, axis=1) for x in below]
-        last = [pltpu.roll(u, LANES - 8, axis=1) for u in us]
-        for f in range(bins):
-            work[f, 0 : size - 8, :] = below[f]
-            work[f, size - 8 : size, :] = last[f]
-        return carry
-
-    lax.fori_loop(0, size // 8, body, 0)
+        coming = panels([pltpu.roll(x, LANES - 8, axis=1) for x in heads])
+        store(us, updates)
+        return tuple(coming)
+
+    us = lax.fori_loop(0, size // 8 - 1, body, tuple(panels([work[f, 0:8, :] for f in range(bins)])))
+    store(us, None)
     if size < LANES:
         for f in range(bins):
             work[f, 0:size, :] = pltpu.roll(work[f, 0:size, :], size, axis=1)

time: 97.8 us -> 91.7 us (0.938)
  Pallas kernels: 93 us -> 86.9 us
    pallas_call x1, Pallas kernels: 45.6 us -> 39.5 us  [solve(): pl.pallas_call(functools.partial(solve_kernel, bins), out_shape=jax.Shape...]
where the time goes in v2:
time: 91.7 us; the launch traced here: 91.5 us
  Pallas kernels  86.9 us (95%)
  local copies, waits for them, and re-layouts  2.14 us (2%)
  other arithmetic  1.81 us (2%)
    pallas_call x1, Pallas kernels, solve(): pl.pallas_call(functools.partial(solve_kernel, bins), out_shape=jax.Shape...  39.5 us
    pallas_call x1, Pallas kernels, summed_cov(): pl.pallas_call(functools.partial(cov_kernel, n, chunk), out_shape=jax.Sha...  33.5 us
    pallas_call x1, Pallas kernels, parcel_power(): pl.pallas_call(functools.partial(parcel_kernel, nf, ns), out_shape=jax.Sh...  13.9 us
    unnamed x3, local copies, waits for them, and re-layouts  1.87 us

profile of v2, /device:TPU:0, one launch (start us, length us, event | category | flops | bytes accessed | tf_op | source)
XLA Modules:
  0.0 91.5 jit_solution(2200596413321263395)
XLA Ops:
  0.6 0.0 copy-start
  0.6 0.6 copy-done
  1.3 0.1 pad.3.clone
  1.4 1.0 %broadcast_multiply_fusion = bf16[2,2,306,64]{2,3,1,0:T(8,128)(2,1)S(1)} fusion(bf16[2,2,306,64]{2,3,1,0:T(8,128)(2,1)} %param.4, bf16[64]{0:T(256)(128)(2,1)S(1)} %convert_element_type.3), kind=kLoop, calls=%fused_computation.1 | loop fusion | flops 78336 | bytes 313472 | tf_op jit(solution)/shard_map/mul | solution.py:370
  2.4 0.2 copy.7
  2.6 0.8 maximum_maximum_fusion.x_ref
  3.4 33.5 %cov_exchange.1.packed_ref = f32[144,8,128]{2,1,0:T(8,128)} custom-call(bf16[2,320,128]{2,1,0:T(8,128)(2,1)} %maximum_maximum_fusion.x_ref), custom_call_target="tpu_custom_call" | custom-call | tf_op jit(solution)/shard_map/cov_exchange/pallas_call | solution.py:92
  36.9 39.5 %factor_whiten.1.power_ref = f32[2,256]{1,0:T(2,128)} custom-call(f32[144,8,128]{2,1,0:T(8,128)} %cov_exchange.1.packed_ref, f32[3,306,256]{2,1,0:T(8,128)} %lead_ref.1), custom_call_target="tpu_custom_call" | custom-call | tf_op jit(solution)/shard_map/factor_whiten/pallas_call | solution.py:273
  76.4 13.9 %parcel_exchange.1 = f32[2,68]{1,0:T(2,128)} custom-call(f32[2,256]{1,0:T(2,128)} %factor_whiten.1.power_ref, s32[1,256]{1,0:T(1,128)} %bitcast.5), custom_call_target="tpu_custom_call" | custom-call | tf_op jit(solution)/shard_map/parcel_exchange/pallas_call | solution.py:347
  90.3 1.2 %copy.9 = f32[2,68]{1,0:T(2,128)} copy(f32[2,68]{1,0:T(2,128)} %parcel_exchange.1) | data formatting | bytes 1088
  (4 shorter events, 0.0 us)
Async XLA Ops:
  0.6 0.7 copy-start

commit v3 on v2

--- a/solution.py
+++ b/solution.py
@@ -23,11 +23,13 @@
     return sizes, offsets, total
 
 
-def cov_kernel(n, chunk, x_ref, out_ref, packed, landing, gathered, send, recv, send2, recv2):
+def exchange_cov(nf, n, chunk, x_ref, packed, landing, gathered, send, recv, send2, recv2):
     bins, rows, _ = x_ref.shape
     sizes, offsets, total = block_plan(rows)
-    me = lax.axis_index("src")
+    me, mf = lax.axis_index("src"), lax.axis_index("freq")
     barrier = pltpu.get_barrier_semaphore()
+    for d in range(1, nf):
+        pl.semaphore_signal(barrier, inc=1, device_id={"freq": lax.rem(mf + d, nf)}, device_id_type=MESH)
     for d in range(1, n):
         pl.semaphore_signal(barrier, inc=1, device_id={"src": lax.rem(me + d, n)}, device_id_type=MESH)
     for f in range(bins):
@@ -44,7 +46,7 @@
     spare = n * chunk - bins * total
     if spare:
         packed[bins * total :] = jnp.zeros((spare, 8, LANES), jnp.float32)
-    pl.semaphore_wait(barrier, n - 1)
+    pl.semaphore_wait(barrier, nf + n - 2)
     copies = []
     for d in range(1, n):
         to = lax.rem(me + d, n)
@@ -81,31 +83,6 @@
     for d in range(1, n):
         copies[d - 1].wait_send()
         again[d - 1].wait_send()
-    out_ref[...] = gathered[...]
-
-
-def summed_cov(x, n):
-    bins, rows, _ = x.shape
-    total = block_plan(rows)[2] * bins
-    chunk = -(-total // n)
-    full = (n * chunk, 8, LANES)
-    return pl.pallas_call(
-        functools.partial(cov_kernel, n, chunk),
-        out_shape=jax.ShapeDtypeStruct(full, jnp.float32),
-        in_specs=[pl.BlockSpec(memory_space=pltpu.VMEM)],
-        out_specs=pl.BlockSpec(memory_space=pltpu.VMEM),
-        scratch_shapes=[
-            pltpu.VMEM(full, jnp.float32),
-            pltpu.VMEM((n, chunk, 8, LANES), jnp.float32),
-            pltpu.VMEM(full, jnp.float32),
-            pltpu.SemaphoreType.DMA((n,)),
-            pltpu.SemaphoreType.DMA((n,)),
-            pltpu.SemaphoreType.DMA((n,)),
-            pltpu.SemaphoreType.DMA((n,)),
-        ],
-        compiler_params=pltpu.CompilerParams(collective_id=0, has_side_effects=True),
-        name="cov_exchange",
-    )(x)
 
 
 def split3(x):
@@ -265,38 +242,12 @@
     return -(-(channels + 1) // 16) * 16
 
 
-def solve(packed, lead_field, bins):
-    channels, sources = lead_field.shape[1:]
-    rows = blocks_rows(channels)
-    sizes, _, _ = block_plan(rows)
-    count = len(sizes)
-    return pl.pallas_call(
-        functools.partial(solve_kernel, bins),
-        out_shape=jax.ShapeDtypeStruct((bins, sources), jnp.float32),
-        in_specs=[pl.BlockSpec(memory_space=pltpu.VMEM)] * 2,
-        out_specs=pl.BlockSpec(memory_space=pltpu.VMEM),
-        scratch_shapes=[
-            pltpu.VMEM((bins, count, count, LANES, LANES), jnp.float32),
-            pltpu.VMEM((bins, LANES, LANES), jnp.float32),
-            pltpu.VMEM((bins, rows, 3 * sources), jnp.float32),
-            pltpu.VMEM((sizes[-1], 3 * sources), jnp.float32),
-        ],
-        name="factor_whiten",
-    )(packed, lead_field)
-
-
-def parcel_kernel(nf, ns, power_ref, parcel_ref, out_ref, mine, bin_land, part, part_land, send_f, recv_f, send_s, recv_s):
+def exchange_parcels(nf, ns, power_ref, parcel_ref, out_ref, mine, bin_land, part, part_land, send_f, recv_f, send_s, recv_s):
     bins, sources = power_ref.shape
     mf, ms = lax.axis_index("freq"), lax.axis_index("src")
-    barrier = pltpu.get_barrier_semaphore()
-    for d in range(1, nf):
-        pl.semaphore_signal(barrier, inc=1, device_id={"freq": lax.rem(mf + d, nf)}, device_id_type=MESH)
-    for d in range(1, ns):
-        pl.semaphore_signal(barrier, inc=1, device_id={"src": lax.rem(ms + d, ns)}, device_id_type=MESH)
     power = power_ref[...]
     here = jnp.sum(power, axis=0, keepdims=True)
     mine[...] = jnp.broadcast_to(here, mine.shape)
-    pl.semaphore_wait(barrier, nf + ns - 2)
     copies = []
     for d in range(1, nf):
         copy = pltpu.make_async_remote_copy(
@@ -342,26 +293,58 @@
     out_ref[...] = whole[0:bins, 0:PARCELS] / whole[bins : bins + 1, 0:PARCELS]
 
 
-def parcel_power(power, parcel, nf, ns):
-    bins, sources = power.shape
+def whole_kernel(nf, ns, chunk, x_ref, lead_hbm, parcel_ref, power_ref, out_ref, lead, lead_sem, *scratch):
+    load = pltpu.make_async_copy(lead_hbm, lead, lead_sem)
+    load.start()
+    exchange_cov(nf, ns, chunk, x_ref, *scratch[:7])
+    load.wait()
+    solve_kernel(x_ref.shape[0], scratch[2], lead, power_ref, *scratch[7:11])
+    exchange_parcels(nf, ns, power_ref, parcel_ref, out_ref, *scratch[11:])
+
+
+def beamform(x, lead_field, parcel, nf, ns):
+    channels, sources = lead_field.shape[1:]
+    bins, rows, _ = x.shape
+    sizes, _, total = block_plan(rows)
+    count = len(sizes)
+    chunk = -(-bins * total // ns)
+    full = (ns * chunk, 8, LANES)
+    dma = pltpu.SemaphoreType.DMA
+    vmem = pl.BlockSpec(memory_space=pltpu.VMEM)
     return pl.pallas_call(
-        functools.partial(parcel_kernel, nf, ns),
-        out_shape=jax.ShapeDtypeStruct((bins, PARCELS), jnp.float32),
-        in_specs=[pl.BlockSpec(memory_space=pltpu.VMEM)] * 2,
-        out_specs=pl.BlockSpec(memory_space=pltpu.VMEM),
+        functools.partial(whole_kernel, nf, ns, chunk),
+        out_shape=[
+            jax.ShapeDtypeStruct((bins, sources), jnp.float32),
+            jax.ShapeDtypeStruct((bins, PARCELS), jnp.float32),
+        ],
+        in_specs=[vmem, pl.BlockSpec(memory_space=pl.ANY), vmem],
+        out_specs=[vmem, vmem],
         scratch_shapes=[
+            pltpu.VMEM(lead_field.shape, jnp.float32),
+            dma(()),
+            pltpu.VMEM(full, jnp.float32),
+            pltpu.VMEM((ns, chunk, 8, LANES), jnp.float32),
+            pltpu.VMEM(full, jnp.float32),
+            dma((ns,)),
+            dma((ns,)),
+            dma((ns,)),
+            dma((ns,)),
+            pltpu.VMEM((bins, count, count, LANES, LANES), jnp.float32),
+            pltpu.VMEM((bins, LANES, LANES), jnp.float32),
+            pltpu.VMEM((bins, rows, 3 * sources), jnp.float32),
+            pltpu.VMEM((sizes[-1], 3 * sources), jnp.float32),
             pltpu.VMEM((8, sources), jnp.float32),
             pltpu.VMEM((nf, 8, sources), jnp.float32),
             pltpu.VMEM((8, LANES), jnp.float32),
             pltpu.VMEM((ns, 8, LANES), jnp.float32),
-            pltpu.SemaphoreType.DMA((nf,)),
-            pltpu.SemaphoreType.DMA((nf,)),
-            pltpu.SemaphoreType.DMA((ns,)),
-            pltpu.SemaphoreType.DMA((ns,)),
+            dma((nf,)),
+            dma((nf,)),
+            dma((ns,)),
+            dma((ns,)),
         ],
-        compiler_params=pltpu.CompilerParams(collective_id=1, has_side_effects=True),
-        name="parcel_exchange",
-    )(power, parcel)
+        compiler_params=pltpu.CompilerParams(collective_id=0, has_side_effects=True),
+        name="beamform",
+    )(x, lead_field, parcel)
 
 
 def epoch_rows(spectra, keep):
@@ -377,10 +360,8 @@
 
 
 def local(nf, ns, spectra, keep, lead_field, parcel):
-    bins = spectra.shape[0]
-    packed = summed_cov(epoch_rows(spectra, keep), ns)
-    power = solve(packed, lead_field, bins)
-    return power, parcel_power(power, parcel[None, :], nf, ns)
+    power, parcels = beamform(epoch_rows(spectra, keep), lead_field, parcel[None, :], nf, ns)
+    return power, parcels
 
 
 def solution(mesh):

time: 91.7 us -> 88 us (0.960)
  Pallas kernels: 86.9 us -> 82.5 us
    pallas_call x3 -> x1, Pallas kernels: 86.9 us -> 82.5 us  [beamform(): pl.pallas_call(functools.partial(whole_kernel, nf, ns, chunk), out_shape=...]
    unnamed x3 -> x6, local copies, waits for them, and re-layouts: 1.87 us -> 1.84 us
where the time goes in v3:
time: 88 us; the launch traced here: 87.8 us
  Pallas kernels  82.5 us (94%)
  other arithmetic  2.45 us (3%)
  local copies, waits for them, and re-layouts  2.1 us (2%)
    pallas_call x1, Pallas kernels, beamform(): pl.pallas_call(functools.partial(whole_kernel, nf, ns, chunk), out_shape=...  82.5 us
    unnamed x6, local copies, waits for them, and re-layouts  1.84 us

profile of v3, /device:TPU:0, one launch (start us, length us, event | category | flops | bytes accessed | tf_op | source)
XLA Modules:
  0.0 87.8 jit_solution(8523436848656716413)
XLA Ops:
  0.6 0.7 convert_element_type.3
  1.3 1.0 %broadcast_multiply_fusion = bf16[2,2,306,64]{2,3,1,0:T(8,128)(2,1)S(1)} fusion(bf16[2,2,306,64]{2,3,1,0:T(8,128)(2,1)} %param.4, bf16[64]{0:T(256)(128)(2,1)S(1)} %convert_element_type.3), kind=kLoop, calls=%fused_computation.1 | loop fusion | flops 78336 | bytes 313472 | tf_op jit(solution)/shard_map/mul | solution.py:353
  2.3 0.2 copy.7
  2.5 0.1 pad.3.clone
  2.6 0.8 maximum_maximum_fusion.x_ref
  3.4 82.5 %beamform.1 = (f32[2,256]{1,0:T(2,128)}, f32[2,68]{1,0:T(2,128)}) custom-call(bf16[2,320,128]{2,1,0:T(8,128)(2,1)} %maximum_maximum_fusion.x_ref, f32[3,306,256]{2,1,0:T(8,128)} %lead_hbm.1, s32[1,256]{1,0:T(1,128)} %bitcast.5), custom_call_target="tpu_custom_call" | custom-call | tf_op jit(solution)/shard_map/beamform/pallas_call | solution.py:314
  85.9 0.0 copy-start
  85.9 0.6 copy-done
  86.6 0.0 copy-start.1
  86.6 0.6 copy.10
  87.1 0.1 copy-done.1
  87.2 0.6 copy.11
  (3 shorter events, 0.0 us)
Async XLA Ops:
  85.9 0.7 copy-start
  86.6 0.6 copy-start.1

commit v4 on v3

--- a/solution.py
+++ b/solution.py
@@ -95,16 +95,20 @@
 def panels(ps):
     lane = lax.broadcasted_iota(jnp.int32, (8, LANES), 1)
     row = lax.broadcasted_iota(jnp.int32, (8, LANES), 0)
+    spread = [
+        [jnp.where(row >= 0, jnp.broadcast_to(p[:, j : j + 1], (8, LANES)), 0.0) for j in range(8)] for p in ps
+    ]
     for k in range(8):
         done = []
-        for p in ps:
-            col = jnp.where(row >= k, jnp.broadcast_to(p[:, k : k + 1], (8, LANES)), 0.0)
+        for p, cols in zip(ps, spread):
+            col = jnp.where(row >= k, cols[k], 0.0)
             pivot = jnp.broadcast_to(col[k : k + 1, :], (8, LANES))
-            line = jnp.where(lane == k, 1.0, jnp.broadcast_to(p[k : k + 1, :], (8, LANES)))
             scale = lax.rsqrt(pivot)
             scale = scale * (1.5 - (0.5 * pivot) * (scale * scale))
-            line = line * scale
             step = col * scale
+            for j in range(k + 1, 8):
+                cols[j] = cols[j] - step * (jnp.broadcast_to(cols[j][k : k + 1, :], (8, LANES)) * scale)
+            line = jnp.where(lane == k, 1.0, jnp.broadcast_to(p[k : k + 1, :], (8, LANES))) * scale
             below = jnp.where((lane == k) & (row > k), 0.0, p) - step * line
             done.append(jnp.where(row > k, below, jnp.where(row == k, line, p)))
         ps = done

time: 88 us -> 71.4 us (0.81)
  Pallas kernels: 82.5 us -> 66 us
    pallas_call x1, Pallas kernels: 82.5 us -> 66 us  [beamform(): pl.pallas_call(functools.partial(whole_kernel, nf, ns, chunk), out_shape=...]
where the time goes in v4:
time: 71.4 us; the launch traced here: 71.2 us
  Pallas kernels  66 us (92%)
  other arithmetic  2.45 us (3%)
  local copies, waits for them, and re-layouts  2.1 us (3%)
    pallas_call x1, Pallas kernels, beamform(): pl.pallas_call(functools.partial(whole_kernel, nf, ns, chunk), out_shape=...  66 us
    unnamed x6, local copies, waits for them, and re-layouts  1.84 us

profile of v4, /device:TPU:0, one launch (start us, length us, event | category | flops | bytes accessed | tf_op | source)
XLA Modules:
  0.0 71.2 jit_solution(6885202548494454051)
XLA Ops:
  0.6 0.7 convert_element_type.3
  1.3 1.0 %broadcast_multiply_fusion = bf16[2,2,306,64]{2,3,1,0:T(8,128)(2,1)S(1)} fusion(bf16[2,2,306,64]{2,3,1,0:T(8,128)(2,1)} %param.4, bf16[64]{0:T(256)(128)(2,1)S(1)} %convert_element_type.3), kind=kLoop, calls=%fused_computation.1 | loop fusion | flops 78336 | bytes 313472 | tf_op jit(solution)/shard_map/mul | solution.py:357
  2.3 0.2 copy.7
  2.5 0.1 pad.3.clone
  2.6 0.8 %maximum_maximum_fusion.x_ref = bf16[2,320,128]{2,1,0:T(8,128)(2,1)} fusion(bf16[2,1,128]{2,1,0:T(2,128)(2,1)S(1)} %broadcast_in_dim.6, bf16[2,306,128]{2,1,0:T(8,128)(2,1)S(1)} %copy.7, bf16[320]{0:T(512)(128)(2,1)S(1)} %pad.3.clone), kind=kLoop, calls=%fused_computation | loop fusion | flops 491520 | bytes 321664 | tf_op jit(solution)/shard_map/concatenate | solution.py:363
  3.4 66.0 %beamform.1 = (f32[2,256]{1,0:T(2,128)}, f32[2,68]{1,0:T(2,128)}) custom-call(bf16[2,320,128]{2,1,0:T(8,128)(2,1)} %maximum_maximum_fusion.x_ref, f32[3,306,256]{2,1,0:T(8,128)} %lead_hbm.1, s32[1,256]{1,0:T(1,128)} %bitcast.5), custom_call_target="tpu_custom_call" | custom-call | tf_op jit(solution)/shard_map/beamform/pallas_call | solution.py:318
  69.3 0.0 copy-start
  69.4 0.6 copy-done
  70.0 0.0 copy-start.1
  70.0 0.6 copy.10
  70.6 0.1 copy-done.1
  70.6 0.6 copy.11
  (3 shorter events, 0.0 us)
Async XLA Ops:
  69.3 0.7 copy-start
  70.0 0.6 copy-start.1
